TPU v7x, 256 devices: a whole 4x4x8 slice. The times are simulated.
256 devices in a mesh: ctx: 16 (over z, core), exp: 16 (over x, y).
Axes of the slice: x: 4, y: 4, z: 8, core: 2. Of those that a mesh axis runs over, the one named last changes fastest.
Arguments:
- queries: bfloat16 [2, 16384, 2560], P(None, ('ctx', 'exp'))
- key_states: bfloat16 [2, 16384, 512], P(None, ('ctx', 'exp'))
- value_state_rows: bfloat16 [2, 16384, 512], P(None, ('ctx', 'exp')), may hold values from -6 to 6
- block_lists: int32 [32], replicated, may hold values from 0 to 31, as said below
- hidden: bfloat16 [8192, 5120], P(('ctx', 'exp')), may hold values from -8 to 8
- router: bfloat16 [5120, 16], replicated, may hold values from -0.078125 to 0.078125
- expert_ids: int32 [8192, 1], P(('ctx', 'exp')), may hold values from 0 to 15; in each aligned block of 32 rows (0 to 31, 32 to 63, ...) at most 4 rows name the same one
- w_gate: bfloat16 [16, 5120, 4096], P('exp', None, 'ctx'), may hold values from -0.078125 to 0.078125
- w_up: bfloat16 [16, 5120, 4096], P('exp', None, 'ctx'), may hold values from -0.078125 to 0.078125
- w_down: bfloat16 [16, 4096, 5120], P('exp', 'ctx'), may hold values from -0.1875 to 0.1875
Outputs:
- attention: bfloat16 [2, 16384, 2560], P(None, ('ctx', 'exp'))
- moe_out: bfloat16 [8192, 5120], P(('ctx', 'exp'))
Inputs may be any that keep to these rules, and one draw needn't show every extreme that they name: block_lists[b] is a block before b, or b itself when block b attends only to its own keys (always for b = 0 and for b = 31). Block p is held by index min(p, 31 - p) of ctx; for each d < 16 with block_lists[d] != d and block_lists[31 - d] != 31 - d, the two listed blocks are held by different indices. `expert_ids`: among the rows of one device no expert is named more than 4 times.
All inputs are finite; a program needn't handle non-finite values.
Results may differ from a plain program's by a relative error of at most 0.023.
Values may be sent and summed in bfloat16 or wider, within the bound.
No kernel may reach another device: no remote copies, remote signals or barrier semaphores. Data moves between devices by JAX's collectives and lax.ppermute only.
A program may use at most 128 MiB of HBM per device.

v0:
```python
import jax
import jax.numpy as jnp
from jax import lax
from jax.sharding import PartitionSpec as P

QUERY_HEADS = 20
KEY_HEADS = 4
HEAD_DIM = 128
NEGATIVE_LARGE = -1e30


def attend_all(queries, key_states, value_state_rows, block_lists):
    ctx_count = lax.axis_size("ctx")
    blocks_total = 2 * ctx_count
    ctx_index = lax.axis_index("ctx")
    exp_index = lax.axis_index("exp")
    row_total_count = queries.shape[1]
    query_group_width = QUERY_HEADS // KEY_HEADS
    key_value_width = KEY_HEADS * HEAD_DIM
    paired = jnp.concatenate([key_states, value_state_rows], axis=2)
    own_blocks = jnp.stack([ctx_index, blocks_total - 1 - ctx_index])
    listed = block_lists[own_blocks]
    usable = listed != own_blocks
    holder = jnp.minimum(listed, blocks_total - 1 - listed)
    everyone = lax.all_gather(paired[None], "ctx", axis=0, tiled=True)
    second_half = (listed >= ctx_count).astype(jnp.int32)
    remote = everyone[holder, second_half]
    stacked = jnp.concatenate([paired, remote], axis=0)
    query_head_rows = queries.reshape(2, row_total_count, KEY_HEADS, query_group_width, HEAD_DIM)
    query_pos = exp_index * row_total_count + jnp.arange(row_total_count)
    scaling = HEAD_DIM ** (-0.5)
    piece_rows = lax.all_gather(stacked, "exp", axis=1, tiled=True)
    running_maximum = jnp.full(
        (2, KEY_HEADS, query_group_width, row_total_count), NEGATIVE_LARGE, jnp.float32
    )
    key_total_count = piece_rows.shape[1]
    concatenated_rows = jnp.concatenate([piece_rows[0:2], piece_rows[2:4]], axis=1)
    key_portion = concatenated_rows[..., :key_value_width].reshape(
        2, 2 * key_total_count, KEY_HEADS, HEAD_DIM
    )
    value_portion = concatenated_rows[..., key_value_width:].reshape(
        2, 2 * key_total_count, KEY_HEADS, HEAD_DIM
    )
    scores = (
        jnp.einsum(
            "prhgd,pkhd->phgrk", query_head_rows, key_portion, preferred_element_type=jnp.float32
        )
        * scaling
    )
    key_pos = jnp.arange(key_total_count)
    causal = jnp.broadcast_to(
        (key_pos[None, :] <= query_pos[:, None])[None], (2, row_total_count, key_total_count)
    )
    listed_ok = jnp.broadcast_to(usable[:, None, None], (2, row_total_count, key_total_count))
    allowed = jnp.concatenate([causal, listed_ok], axis=2)[:, None, None]
    masked = jnp.where(allowed, scores, NEGATIVE_LARGE)
    new_max = jnp.maximum(running_maximum, jnp.max(masked, axis=-1))
    weights = jnp.where(allowed, jnp.exp(masked - new_max[..., None]), 0.0)
    new_sum = jnp.sum(weights, axis=-1)
    update = jnp.einsum(
        "phgrk,pkhd->phgrd",
        weights.astype(jnp.bfloat16),
        value_portion,
        preferred_element_type=jnp.float32,
    )
    mixed_rows = update / new_sum[..., None]
    return (
        jnp.transpose(mixed_rows, (0, 3, 1, 2, 4))
        .reshape(2, row_total_count, QUERY_HEADS * HEAD_DIM)
        .astype(jnp.bfloat16)
    )


def route_experts(hidden, router, expert_ids, w_gate, w_up, w_down):
    expert_table = router.shape[1]
    local_tokens = hidden.shape[0]
    model_width = hidden.shape[1]
    capacity = max(2, 2 * local_tokens // expert_table)
    exp_count = lax.axis_size("exp")
    logits = jnp.dot(hidden, router, preferred_element_type=jnp.float32)
    selected_expert = expert_ids[:, 0]
    onehot = (selected_expert[:, None] == jnp.arange(expert_table)[None, :]).astype(jnp.float32)
    gate_score = jax.nn.sigmoid(jnp.sum(logits * onehot, axis=1))
    scaled_scores = (hidden.astype(jnp.float32) * gate_score[:, None]).astype(jnp.bfloat16)
    slot_rank = (jnp.sum(jnp.cumsum(onehot, axis=0) * onehot, axis=1) - 1.0).astype(jnp.int32)
    dispatch = (
        (selected_expert[None, None, :] == jnp.arange(expert_table)[:, None, None])
        & (slot_rank[None, None, :] == jnp.arange(capacity)[None, :, None])
    ).astype(jnp.bfloat16)
    gate_local = w_gate[0]
    up_local = w_up[0]
    down_local = w_down[0]
    outgoing = jnp.einsum(
        "ect,td->ecd", dispatch, scaled_scores, preferred_element_type=jnp.float32
    ).astype(jnp.bfloat16)
    incoming = lax.all_to_all(outgoing, "exp", split_axis=0, concat_axis=0, tiled=True)
    piece_rows = lax.all_gather(incoming.reshape(-1, model_width), "ctx", axis=0, tiled=True)
    gate_part = jnp.dot(piece_rows, gate_local, preferred_element_type=jnp.float32)
    up_part = jnp.dot(piece_rows, up_local, preferred_element_type=jnp.float32)
    hidden_activation = (jax.nn.silu(gate_part) * up_part).astype(jnp.bfloat16)
    summed_output = lax.psum_scatter(
        jnp.dot(hidden_activation, down_local, preferred_element_type=jnp.float32).astype(
            jnp.bfloat16
        ),
        "ctx",
        scatter_dimension=0,
        tiled=True,
    )
    returned = lax.all_to_all(
        summed_output.reshape(exp_count, capacity, model_width),
        "exp",
        split_axis=0,
        concat_axis=0,
        tiled=True,
    )
    return jnp.einsum("ect,ecd->td", dispatch, returned, preferred_element_type=jnp.float32).astype(
        jnp.bfloat16
    )


def shards(
    queries,
    key_states,
    value_state_rows,
    block_lists,
    hidden,
    router,
    expert_ids,
    w_gate,
    w_up,
    w_down,
):
    attention = attend_all(queries, key_states, value_state_rows, block_lists)
    moe_out = route_experts(hidden, router, expert_ids, w_gate, w_up, w_down)
    return (attention, moe_out)


def solution(mesh):
    placed = (
        P(None, ("ctx", "exp"), None),
        P(None, ("ctx", "exp"), None),
        P(None, ("ctx", "exp"), None),
        P(),
        P(("ctx", "exp"), None),
        P(),
        P(("ctx", "exp"), None),
        P("exp", None, "ctx"),
        P("exp", None, "ctx"),
        P("exp", "ctx", None),
    )
    return jax.shard_map(
        shards,
        mesh=mesh,
        in_specs=placed,
        out_specs=(P(None, ("ctx", "exp"), None), P(("ctx", "exp"), None)),
        check_vma=False,
    )
```

profile of v0, /device:TPU:2, one launch (start us, length us, event | category | flops | bytes accessed | tf_op | source)
XLA Modules:
  0.0 308.0 jit_solution(14980662462300857561)
XLA Ops:
  7.2 0.0 all-gather.9.cloned.1.call-start
  7.2 1.1 constant_dynamic-update-slice_fusion.1
  8.3 0.9 constant_dynamic-update-slice_fusion
  9.2 0.7 copy-done.2
  9.9 0.0 all-gather.9.cloned.1.call-update
  9.9 0.0 all-gather.7.cloned.1.call-start
  10.0 0.7 fusion.45
  10.7 0.1 copy.28
  10.7 0.1 reduce_window_sum.11
  10.8 0.1 copy.29
  10.9 0.7 select_reduce_fusion
  11.5 1.3 fusion.24
  12.9 0.7 iota_compare_fusion.2
  13.5 1.4 convolution_convert_fusion.1
  14.9 0.5 copy.30
  15.4 18.6 %all_to_all.10 = bf16[16,4,5120]{2,1,0:T(4,128)(2,1)S(1)} all-to-all(bf16[16,4,5120]{2,1,0:T(4,128)(2,1)S(1)} %copy.30), channel_id=1, replica_groups=mesh['ctx'=16,'exp'=16] {'exp'}, dimensions={0} | all-to-all | bytes 1310720 | tf_op jit(solution)/shard_map/all_to_all | solution.py:96
  34.0 1.0 reshape.252
  35.0 0.0 all-gather.7.cloned.1.call-update
  35.0 0.0 all-gather.5.cloned.1.call-start
  35.1 0.1 fusion.46
  35.2 1.3 gather_fusion
  36.5 19.3 %all-gather.9.cloned.1.call-done = bf16[32,64,1024]{2,1,0:T(8,128)(2,1)} async-done(((bf16[2,64,1024]{2,1,0:T(8,128)(2,1)}), bf16[32,64,1024]{2,1,0:T(8,128)(2,1)}) %all-gather.9.cloned.1.call-update) | async-done | bytes 4194320 | tf_op jit(solution)/shard_map/all_gather | solution.py:25
  55.8 2.8 gather_fusion.1
  58.5 1.8 pad_maximum_fusion.1
  60.3 0.0 all-gather.5.cloned.1.call-update
  60.3 0.0 reduce-scatter.2.cloned.1.call-start
  60.4 61.9 %all-gather.7.cloned.1.call-done = bf16[1024,5120]{1,0:T(8,128)(2,1)} async-done(((bf16[64,5120]{1,0:T(8,128)(2,1)}), bf16[1024,5120]{1,0:T(8,128)(2,1)}) %all-gather.7.cloned.1.call-update) | async-done | bytes 10485776 | tf_op jit(solution)/shard_map/all_gather | solution.py:97
  122.3 8.6 %fusion.11 = f32[1024,256]{1,0:T(8,128)} fusion(bf16[1024,5120]{1,0:T(8,128)(2,1)} %all-gather.7.cloned.1.call-done, bf16[1,5120,256]{2,1,0:T(8,128)(2,1)} %param.17), kind=kOutput, calls=%fused_computation.20 | convolution fusion | flops 2684354560 | bytes 14155776 | tf_op jit(solution)/shard_map/dot_general | solution.py:98
  130.9 21.1 %convolution_convert_fusion = bf16[1024,5120]{1,0:T(8,128)(2,1)} fusion(bf16[1,256,5120]{2,1,0:T(8,128)(2,1)S(1)} %copy-done, bf16[1024,5120]{1,0:T(8,128)(2,1)} %all-gather.7.cloned.1.call-done, bf16[1,5120,256]{2,1,0:T(8,128)(2,1)} %param.18, f32[1024,256]{1,0:T(8,128)} %fusion.11), kind=kOutput, calls=%fused_computation.9 | convolution fusion | flops 5375524864 | bytes 27262976 | tf_op jit(solution)/shard_map/dot_general | solution.py:102
  152.0 1.1 copy-done.3
  153.1 0.8 reshape.250
  153.9 0.1 add_compare_fusion
  153.9 0.1 iota_compare_fusion
  154.1 0.1 broadcast_in_dim.27
  154.2 44.9 %all-gather.5.cloned.1.call-done = bf16[4,1024,1024]{2,1,0:T(8,128)(2,1)} async-done(((bf16[4,64,1024]{2,1,0:T(8,128)(2,1)}), bf16[4,1024,1024]{2,1,0:T(8,128)(2,1)}) %all-gather.5.cloned.1.call-update) | async-done | bytes 8388624 | tf_op jit(solution)/shard_map/all_gather | solution.py:32
  199.1 3.9 %fusion.57 = (bf16[2,1024,1024]{2,1,0:T(8,128)(2,1)S(1)}, bf16[2,1024,1024]{2,1,0:T(8,128)(2,1)S(1)}) fusion(bf16[4,1024,1024]{2,1,0:T(8,128)(2,1)} %all-gather.5.cloned.1.call-done), kind=kLoop, calls=%fused_computation.78 | loop fusion | bytes 16777216 | tf_op jit(solution)/shard_map/slice | solution.py:37
  203.1 3.7 %fusion.7 = (bf16[2,2048,512]{2,1,0:T(8,128)(2,1)}, bf16[2,2048,512]{2,1,0:T(8,128)(2,1)}) fusion(bf16[2,1024,1024]{2,1,0:T(8,128)(2,1)S(1)} %get-tuple-element.4, bf16[2,1024,1024]{2,1,0:T(8,128)(2,1)S(1)} %get-tuple-element.5), kind=kLoop, calls=%fused_computation.15 | loop fusion | flops 16777216 | bytes 16777216 | tf_op jit(solution)/shard_map/concatenate | solution.py:37
  206.8 6.3 %copy.25 = bf16[2,2048,512]{1,2,0:T(8,128)(2,1)} copy(bf16[2,2048,512]{2,1,0:T(8,128)(2,1)} %get-tuple-element.3) | data formatting | bytes 8388608 | tf_op jit(solution)/shard_map/slice | solution.py:41
  213.1 6.3 %copy.22 = bf16[2,2048,512]{1,2,0:T(8,128)(2,1)} copy(bf16[2,2048,512]{2,1,0:T(8,128)(2,1)} %get-tuple-element.2) | data formatting | bytes 8388608 | tf_op jit(solution)/shard_map/slice | solution.py:38
  219.4 13.4 %fusion = (f32[2,4,5,64]{3,2,1,0:T(8,128)S(1)}, f32[2,4,2048,64,5]{2,3,4,1,0:T(8,128)}) fusion(pred[2,64,2048]{2,1,0:T(8,128)(4,1)S(1)} %pad_add_fusion, bf16[2,2048,4,128,1]{1,3,4,2,0:T(8,128)(2,1)} %bitcast.70, bf16[2,64,4,5,128]{4,3,2,1,0:T(8,128)(2,1)S(1)} %reshape.250), kind=kOutput, calls=%fused_computation.4 | convolution fusion | flops 1357903360 | bytes 26093568 | tf_op jit(solution)/shard_map/prhgd,pkhd->phgrk/dot_general | solution.py:45
  232.9 11.6 %fusion.1 = f32[2,4,5,64]{3,2,1,0:T(8,128)} fusion(f32[2,4,2048,64,5]{2,3,4,1,0:T(8,128)} %get-tuple-element.7, f32[2,4,5,64]{3,2,1,0:T(8,128)S(1)} %broadcast_maximum_fusion, pred[2,64,2048]{2,1,0:T(8,128)(4,1)S(1)} %pad_add_fusion), kind=kLoop, calls=%fused_computation.5 | loop fusion | flops 26211840 | bytes 21254144 | tf_op jit(solution)/shard_map/reduce_sum | solution.py:59
  244.5 31.3 %reduce-scatter.2.cloned.1.call-done = bf16[64,5120]{1,0:T(8,128)(2,1)} async-done(((bf16[1024,5120]{1,0:T(8,128)(2,1)}), bf16[64,5120]{1,0:T(8,128)(2,1)}) %reduce-scatter.2.cloned.1.call-update) | async-done | bytes 655376 | tf_op jit(solution)/shard_map/reduce_scatter | solution.py:101
  275.8 2.4 reshape.253
  278.2 7.4 %all-to-all-start.1 = ((bf16[16,4,5120]{2,1,0:T(4,128)(2,1)}), bf16[16,4,5120]{2,1,0:T(4,128)(2,1)S(1)}, u32[]{:S(2)}, u32[]{:S(2)}) async-start(bf16[16,4,5120]{2,1,0:T(4,128)(2,1)} %reshape.253), calls=%async_computation.2 | async-start | bytes 1310720 | tf_op jit(solution)/shard_map/all_to_all | solution.py:109
  285.5 10.9 %divide_convert_fusion = bf16[2,64,4,5,128]{4,1,3,2,0:T(8,128)(2,1)S(1)} fusion(bf16[2,2048,4,128,1]{1,3,4,2,0:T(8,128)(2,1)} %bitcast.71, f32[2,4,2048,64,5]{2,3,4,1,0:T(8,128)} %get-tuple-element.7, f32[2,4,5,64]{3,2,1,0:T(8,128)} %copy-done.4, pred[2,64,2048]{2,1,0:T(8,128)(4,1)S(1)} %pad_add_fusion, f32[2,64,4,5]{1,3,2,0:T(8,128)} %bitcast.72), kind=kOutput, calls=%fused_computation.23 | convolution fusion | flops 1369047040 | bytes 26103808 | tf_op jit(solution)/shard_map/phgrk,pkhd->phgrd/dot_general | solution.py:60
  296.4 1.4 copy.27
  297.9 2.6 convert_element_type.51
  300.4 1.0 fusion.6
  (19 shorter events, 0.1 us)
Async XLA Ops:
  7.2 123.7 %copy-start = (bf16[1,256,5120]{2,1,0:T(8,128)(2,1)S(1)}, bf16[1,256,5120]{2,1,0:T(8,128)(2,1)}, u32[]{:S(2)}) copy-start(bf16[1,256,5120]{2,1,0:T(8,128)(2,1)} %param.19) | copy-start | bytes 7864324
  7.2 48.6 %all-gather.9.cloned.1.call-start = ((), (), s32[]{:S(2)}) async-start(), calls=%async_computation.6 | async-start | bytes 4456448 | tf_op jit(solution)/shard_map/all_gather | solution.py:25
  9.2 0.7 copy-start.2
  9.9 112.4 %all-gather.7.cloned.1.call-start = ((), (), s32[]{:S(2)}) async-start(), calls=%async_computation.4 | async-start | bytes 11141120 | tf_op jit(solution)/shard_map/all_gather | solution.py:97
  35.0 164.1 %all-gather.5.cloned.1.call-start = ((), (), s32[]{:S(2)}) async-start(), calls=%async_computation.3 | async-start | bytes 8912896 | tf_op jit(solution)/shard_map/all_gather | solution.py:32
  60.3 215.5 %reduce-scatter.2.cloned.1.call-start = ((), (), s32[]{:S(2)}) async-start(), calls=%async_computation.5 | async-start | bytes 11141120 | tf_op jit(solution)/shard_map/reduce_scatter | solution.py:101
  152.0 1.1 copy-start.3
  232.9 11.6 %copy-start.4 = (f32[2,4,5,64]{3,2,1,0:T(8,128)}, f32[2,4,5,64]{3,2,1,0:T(8,128)S(1)}, u32[]{:S(2)}) copy-start(f32[2,4,5,64]{3,2,1,0:T(8,128)S(1)} %broadcast_maximum_fusion) | copy-start | bytes 30724
  278.2 22.3 %all-to-all-start.1 = ((bf16[16,4,5120]{2,1,0:T(4,128)(2,1)}), bf16[16,4,5120]{2,1,0:T(4,128)(2,1)S(1)}, u32[]{:S(2)}, u32[]{:S(2)}) async-start(bf16[16,4,5120]{2,1,0:T(4,128)(2,1)} %reshape.253), calls=%async_computation.2 | async-start | bytes 1310720 | tf_op jit(solution)/shard_map/all_to_all | solution.py:109
  285.5 15.9 %copy-start.1 = (bf16[1,256,5120]{2,1,0:T(8,128)(2,1)S(1)}, bf16[1,256,5120]{2,1,0:T(8,128)(2,1)}, u32[]{:S(2)}) copy-start(bf16[1,256,5120]{2,1,0:T(8,128)(2,1)} %param.19) | copy-start | bytes 7864324
Sparse Core Ops, SparseCore 0:
  10.4 45.3 all-gather.8
  58.2 64.0 all-gather.6
  124.8 74.2 all-gather.4
  201.5 74.1 reduce-scatter.1
where the time goes:
time: 309 us; the launch traced here: 308 us
  waiting for transfers between devices  157 us (51%)
  matrix products  57.7 us (19%)
  local copies, waits for them, and re-layouts  33.3 us (11%)
  other arithmetic  19.5 us (6%)
  blocking collectives  18.6 us (6%)
  between operations  13.9 us (4%)
  starting transfers between devices  7.54 us (2%)
    all_gather x1, waiting for transfers between devices, route_experts(): lax.all_gather(incoming.reshape(-1, model_width), 'ctx', axis=0, tiled=True)  61.9 us
    all_gather x1, waiting for transfers between devices, attend_all(): piece_rows = lax.all_gather(stacked, 'exp', axis=1, tiled=True)  44.9 us
    reduce_scatter x1, waiting for transfers between devices, route_experts(): lax.psum_scatter(jnp.dot(hidden_activation, down_local, preferred_element...  31.3 us
    dot_general x1, matrix products, route_experts(): jnp.dot(hidden_activation, down_local, preferred_element_type=jnp.float32)  21.1 us
    all_gather x1, waiting for transfers between devices, attend_all(): everyone = lax.all_gather(paired[None], 'ctx', axis=0, tiled=True)  19.3 us
    all_to_all x1, blocking collectives, route_experts(): lax.all_to_all(outgoing, 'exp', split_axis=0, concat_axis=0, tiled=True)  18.6 us
    dot_general x1, matrix products, attend_all(): jnp.einsum('prhgd,pkhd->phgrk', query_head_rows, key_portion, preferred_e...  13.4 us
    reduce_sum x1, other arithmetic, attend_all(): new_sum = jnp.sum(weights, axis=-1)  11.6 us
  transfers between devices with their start and end apart: 5, of which 4 were waited for; matrix products, arithmetic and copies ran while one was open for 34% of the time, Pallas kernels for 0%

commit v1 on v0

--- a/solution.py
+++ b/solution.py
@@ -7,6 +7,12 @@
 KEY_HEADS = 4
 HEAD_DIM = 128
 NEGATIVE_LARGE = -1e30
+
+
+def gather_from_all(x, axis, dim):
+    peers = lax.axis_size(axis)
+    repeats = [peers if d == dim else 1 for d in range(x.ndim)]
+    return lax.all_to_all(jnp.tile(x, repeats), axis, split_axis=dim, concat_axis=dim, tiled=True)
 
 
 def attend_all(queries, key_states, value_state_rows, block_lists):
@@ -22,7 +28,7 @@
     listed = block_lists[own_blocks]
     usable = listed != own_blocks
     holder = jnp.minimum(listed, blocks_total - 1 - listed)
-    everyone = lax.all_gather(paired[None], "ctx", axis=0, tiled=True)
+    everyone = gather_from_all(paired[None], "ctx", 0)
     second_half = (listed >= ctx_count).astype(jnp.int32)
     remote = everyone[holder, second_half]
     stacked = jnp.concatenate([paired, remote], axis=0)

time: 309 us -> 375 us (1.21)
  waiting for transfers between devices: 157 us -> 215 us
  starting transfers between devices: 7.54 us -> 16.1 us
    all_to_all x0 -> x1, waiting for transfers between devices: none -> 133 us  [gather_from_all(): lax.all_to_all(jnp.tile(x, repeats), axis, split_axis=dim, concat_axis=di...]
    all_gather x1, waiting for transfers between devices: 61.9 us -> 5.62 us  [route_experts(): lax.all_gather(incoming.reshape(-1, model_width), 'ctx', axis=0, tiled=True)]
    all_gather x1 -> x0, waiting for transfers between devices: 19.3 us -> none  [attend_all(): everyone = lax.all_gather(paired[None], 'ctx', axis=0, tiled=True)]
    all_to_all x0 -> x1, starting transfers between devices: none -> 8.63 us  [gather_from_all(): lax.all_to_all(jnp.tile(x, repeats), axis, split_axis=dim, concat_axis=di...]
  transfers between devices with their start and end apart: 5 -> 5, of which waited for: 4 -> 4; matrix products, arithmetic and copies ran while one was open for 34% -> 27% of each run, Pallas kernels for 0% -> 0%
where the time goes in v1:
time: 375 us; the launch traced here: 374 us
  waiting for transfers between devices  215 us (57%)
  matrix products  57.8 us (15%)
  local copies, waits for them, and re-layouts  34.3 us (9%)
  other arithmetic  18.7 us (5%)
  blocking collectives  18.6 us (5%)
  starting transfers between devices  16.1 us (4%)
  between operations  13.9 us (4%)
    all_to_all x1, waiting for transfers between devices, gather_from_all(): lax.all_to_all(jnp.tile(x, repeats), axis, split_axis=dim, concat_axis=di...  133 us
    all_gather x1, waiting for transfers between devices, attend_all(): piece_rows = lax.all_gather(stacked, 'exp', axis=1, tiled=True)  44.6 us
    reduce_scatter x1, waiting for transfers between devices, route_experts(): lax.psum_scatter(jnp.dot(hidden_activation, down_local, preferred_element...  31.5 us
    dot_general x1, matrix products, route_experts(): jnp.dot(hidden_activation, down_local, preferred_element_type=jnp.float32)  21.2 us
    all_to_all x1, blocking collectives, route_experts(): lax.all_to_all(outgoing, 'exp', split_axis=0, concat_axis=0, tiled=True)  18.6 us
    dot_general x1, matrix products, attend_all(): jnp.einsum('prhgd,pkhd->phgrk', query_head_rows, key_portion, preferred_e...  13.5 us
    reduce_sum x1, other arithmetic, attend_all(): new_sum = jnp.sum(weights, axis=-1)  11.6 us
    dot_general x1, matrix products, attend_all(): jnp.einsum('phgrk,pkhd->phgrd', weights.astype(jnp.bfloat16), value_porti...  10.9 us
  transfers between devices with their start and end apart: 5, of which 4 were waited for; matrix products, arithmetic and copies ran while one was open for 27% of the time, Pallas kernels for 0%

profile of v1, /device:TPU:2, one launch (start us, length us, event | category | flops | bytes accessed | tf_op | source)
XLA Modules:
  0.0 374.4 jit_solution(7002491030464252058)
XLA Ops:
  7.2 0.0 all-gather.5.cloned.1.call-start
  7.2 0.8 fusion.45
  8.0 0.7 iota_compare_fusion.2
  8.7 1.3 fusion.24
  10.0 0.1 copy.28
  10.1 0.1 reduce_window_sum.11
  10.1 0.1 copy.29
  10.2 0.7 select_reduce_fusion
  10.9 1.4 convolution_convert_fusion.1
  12.3 0.5 copy.30
  12.8 18.6 %all_to_all.15 = bf16[16,4,5120]{2,1,0:T(4,128)(2,1)S(1)} all-to-all(bf16[16,4,5120]{2,1,0:T(4,128)(2,1)S(1)} %copy.30), channel_id=1, replica_groups=mesh['ctx'=16,'exp'=16] {'exp'}, dimensions={0} | all-to-all | bytes 1310720 | tf_op jit(solution)/shard_map/all_to_all | solution.py:102
  31.4 1.0 reshape.255
  32.4 0.0 all-gather.5.cloned.1.call-update
  32.4 0.9 constant_dynamic-update-slice_fusion.1
  33.3 0.9 constant_dynamic-update-slice_fusion
  34.3 2.5 tile.2
  36.8 8.6 %all-to-all-start = ((bf16[16,2,64,1024]{3,2,1,0:T(8,128)(2,1)}), bf16[16,2,64,1024]{3,2,1,0:T(8,128)(2,1)}, u32[]{:S(2)}, u32[]{:S(2)}) async-start(bf16[16,2,64,1024]{3,2,1,0:T(8,128)(2,1)} %tile.2), calls=%async_computation | async-start | bytes 8388608 | tf_op jit(solution)/shard_map/all_to_all | solution.py:15
  45.4 0.0 all-gather.3.cloned.1.call-start
  45.4 0.1 fusion.46
  45.5 0.6 gather_fusion
  46.2 133.2 %all-to-all-done = bf16[16,2,64,1024]{3,2,1,0:T(8,128)(2,1)} async-done(((bf16[16,2,64,1024]{3,2,1,0:T(8,128)(2,1)}), bf16[16,2,64,1024]{3,2,1,0:T(8,128)(2,1)}, u32[]{:S(2)}, u32[]{:S(2)}) %all-to-all-start) | async-done | bytes 4194336 | tf_op jit(solution)/shard_map/all_to_all | solution.py:15
  179.4 2.8 gather_fusion.1
  182.2 0.8 pad_maximum_fusion.1
  183.1 0.0 all-gather.3.cloned.1.call-update
  183.1 0.0 reduce-scatter.2.cloned.1.call-start
  183.1 5.6 %all-gather.5.cloned.1.call-done = bf16[1024,5120]{1,0:T(8,128)(2,1)} async-done(((bf16[64,5120]{1,0:T(8,128)(2,1)}), bf16[1024,5120]{1,0:T(8,128)(2,1)}) %all-gather.5.cloned.1.call-update) | async-done | bytes 10485776 | tf_op jit(solution)/shard_map/all_gather | solution.py:103
  188.8 8.6 %fusion.11 = f32[1024,256]{1,0:T(8,128)} fusion(bf16[1024,5120]{1,0:T(8,128)(2,1)} %all-gather.5.cloned.1.call-done, bf16[1,5120,256]{2,1,0:T(8,128)(2,1)} %param.17), kind=kOutput, calls=%fused_computation.20 | convolution fusion | flops 2684354560 | bytes 14155776 | tf_op jit(solution)/shard_map/dot_general | solution.py:104
  197.4 21.2 %convolution_convert_fusion = bf16[1024,5120]{1,0:T(8,128)(2,1)} fusion(bf16[1,256,5120]{2,1,0:T(8,128)(2,1)S(1)} %copy-done, bf16[1024,5120]{1,0:T(8,128)(2,1)} %all-gather.5.cloned.1.call-done, bf16[1,5120,256]{2,1,0:T(8,128)(2,1)} %param.18, f32[1024,256]{1,0:T(8,128)} %fusion.11), kind=kOutput, calls=%fused_computation.9 | convolution fusion | flops 5375524864 | bytes 27262976 | tf_op jit(solution)/shard_map/dot_general | solution.py:108
  218.6 0.0 reduce-scatter.2.cloned.1.call-update
  218.6 1.1 copy-done.3
  219.6 0.8 reshape.253
  220.4 0.1 add_compare_fusion
  220.5 0.1 iota_compare_fusion
  220.6 0.1 broadcast_in_dim.25
  220.8 44.6 %all-gather.3.cloned.1.call-done = bf16[4,1024,1024]{2,1,0:T(8,128)(2,1)} async-done(((bf16[4,64,1024]{2,1,0:T(8,128)(2,1)}), bf16[4,1024,1024]{2,1,0:T(8,128)(2,1)}) %all-gather.3.cloned.1.call-update) | async-done | bytes 8388624 | tf_op jit(solution)/shard_map/all_gather | solution.py:38
  265.4 3.9 %fusion.57 = (bf16[2,1024,1024]{2,1,0:T(8,128)(2,1)S(1)}, bf16[2,1024,1024]{2,1,0:T(8,128)(2,1)S(1)}) fusion(bf16[4,1024,1024]{2,1,0:T(8,128)(2,1)} %all-gather.3.cloned.1.call-done), kind=kLoop, calls=%fused_computation.78 | loop fusion | bytes 16777216 | tf_op jit(solution)/shard_map/slice | solution.py:43
  269.3 3.8 %fusion.7 = (bf16[2,2048,512]{2,1,0:T(8,128)(2,1)}, bf16[2,2048,512]{2,1,0:T(8,128)(2,1)}) fusion(bf16[2,1024,1024]{2,1,0:T(8,128)(2,1)S(1)} %get-tuple-element.4, bf16[2,1024,1024]{2,1,0:T(8,128)(2,1)S(1)} %get-tuple-element.5), kind=kLoop, calls=%fused_computation.15 | loop fusion | flops 16777216 | bytes 16777216 | tf_op jit(solution)/shard_map/concatenate | solution.py:43
  273.0 6.2 %copy.25 = bf16[2,2048,512]{1,2,0:T(8,128)(2,1)} copy(bf16[2,2048,512]{2,1,0:T(8,128)(2,1)} %get-tuple-element.3) | data formatting | bytes 8388608 | tf_op jit(solution)/shard_map/slice | solution.py:47
  279.3 6.3 %copy.22 = bf16[2,2048,512]{1,2,0:T(8,128)(2,1)} copy(bf16[2,2048,512]{2,1,0:T(8,128)(2,1)} %get-tuple-element.2) | data formatting | bytes 8388608 | tf_op jit(solution)/shard_map/slice | solution.py:44
  285.6 13.5 %fusion = (f32[2,4,5,64]{3,2,1,0:T(8,128)S(1)}, f32[2,4,2048,64,5]{2,3,4,1,0:T(8,128)}) fusion(pred[2,64,2048]{2,1,0:T(8,128)(4,1)S(1)} %pad_add_fusion, bf16[2,2048,4,128,1]{1,3,4,2,0:T(8,128)(2,1)} %bitcast.69, bf16[2,64,4,5,128]{4,3,2,1,0:T(8,128)(2,1)S(1)} %reshape.253), kind=kOutput, calls=%fused_computation.4 | convolution fusion | flops 1357903360 | bytes 26093568 | tf_op jit(solution)/shard_map/prhgd,pkhd->phgrk/dot_general | solution.py:51
  299.1 11.6 %fusion.1 = f32[2,4,5,64]{3,2,1,0:T(8,128)} fusion(f32[2,4,2048,64,5]{2,3,4,1,0:T(8,128)} %get-tuple-element.7, f32[2,4,5,64]{3,2,1,0:T(8,128)S(1)} %broadcast_maximum_fusion, pred[2,64,2048]{2,1,0:T(8,128)(4,1)S(1)} %pad_add_fusion), kind=kLoop, calls=%fused_computation.5 | loop fusion | flops 26211840 | bytes 21254144 | tf_op jit(solution)/shard_map/reduce_sum | solution.py:65
  310.7 31.5 %reduce-scatter.2.cloned.1.call-done = bf16[64,5120]{1,0:T(8,128)(2,1)} async-done(((bf16[1024,5120]{1,0:T(8,128)(2,1)}), bf16[64,5120]{1,0:T(8,128)(2,1)}) %reduce-scatter.2.cloned.1.call-update) | async-done | bytes 655376 | tf_op jit(solution)/shard_map/reduce_scatter | solution.py:107
  342.2 2.3 reshape.256
  344.5 7.4 %all-to-all-start.2 = ((bf16[16,4,5120]{2,1,0:T(4,128)(2,1)}), bf16[16,4,5120]{2,1,0:T(4,128)(2,1)S(1)}, u32[]{:S(2)}, u32[]{:S(2)}) async-start(bf16[16,4,5120]{2,1,0:T(4,128)(2,1)} %reshape.256), calls=%async_computation.3 | async-start | bytes 1310720 | tf_op jit(solution)/shard_map/all_to_all | solution.py:115
  351.9 10.9 %divide_convert_fusion = bf16[2,64,4,5,128]{4,1,3,2,0:T(8,128)(2,1)S(1)} fusion(bf16[2,2048,4,128,1]{1,3,4,2,0:T(8,128)(2,1)} %bitcast.70, f32[2,4,2048,64,5]{2,3,4,1,0:T(8,128)} %get-tuple-element.7, f32[2,4,5,64]{3,2,1,0:T(8,128)} %copy-done.4, pred[2,64,2048]{2,1,0:T(8,128)(4,1)S(1)} %pad_add_fusion, f32[2,64,4,5]{1,3,2,0:T(8,128)} %bitcast.71), kind=kOutput, calls=%fused_computation.23 | convolution fusion | flops 1369047040 | bytes 26103808 | tf_op jit(solution)/shard_map/phgrk,pkhd->phgrd/dot_general | solution.py:66
  362.8 1.4 copy.27
  364.2 2.6 convert_element_type.51
  366.8 1.0 fusion.6
  (19 shorter events, 0.1 us)
Async XLA Ops:
  7.2 190.2 %copy-start = (bf16[1,256,5120]{2,1,0:T(8,128)(2,1)S(1)}, bf16[1,256,5120]{2,1,0:T(8,128)(2,1)}, u32[]{:S(2)}) copy-start(bf16[1,256,5120]{2,1,0:T(8,128)(2,1)} %param.19) | copy-start | bytes 7864324
  7.2 181.6 %all-gather.5.cloned.1.call-start = ((), (), s32[]{:S(2)}) async-start(), calls=%async_computation.5 | async-start | bytes 11141120 | tf_op jit(solution)/shard_map/all_gather | solution.py:103
  12.8 32.7 %copy-start.2 = (s32[32]{0:T(128)S(1)}, s32[32]{0:T(128)}, u32[]{:S(2)}) copy-start(s32[32]{0:T(128)} %param.13) | copy-start | bytes 388
  36.8 142.7 %all-to-all-start = ((bf16[16,2,64,1024]{3,2,1,0:T(8,128)(2,1)}), bf16[16,2,64,1024]{3,2,1,0:T(8,128)(2,1)}, u32[]{:S(2)}, u32[]{:S(2)}) async-start(bf16[16,2,64,1024]{3,2,1,0:T(8,128)(2,1)} %tile.2), calls=%async_computation | async-start | bytes 8388608 | tf_op jit(solution)/shard_map/all_to_all | solution.py:15
  45.4 220.0 %all-gather.3.cloned.1.call-start = ((), (), s32[]{:S(2)}) async-start(), calls=%async_computation.4 | async-start | bytes 8912896 | tf_op jit(solution)/shard_map/all_gather | solution.py:38
  183.1 159.1 %reduce-scatter.2.cloned.1.call-start = ((), (), s32[]{:S(2)}) async-start(), calls=%async_computation.6 | async-start | bytes 11141120 | tf_op jit(solution)/shard_map/reduce_scatter | solution.py:107
  218.6 1.1 copy-start.3
  299.1 11.6 %copy-start.4 = (f32[2,4,5,64]{3,2,1,0:T(8,128)}, f32[2,4,5,64]{3,2,1,0:T(8,128)S(1)}, u32[]{:S(2)}) copy-start(f32[2,4,5,64]{3,2,1,0:T(8,128)S(1)} %broadcast_maximum_fusion) | copy-start | bytes 30724
  344.5 22.3 %all-to-all-start.2 = ((bf16[16,4,5120]{2,1,0:T(4,128)(2,1)}), bf16[16,4,5120]{2,1,0:T(4,128)(2,1)S(1)}, u32[]{:S(2)}, u32[]{:S(2)}) async-start(bf16[16,4,5120]{2,1,0:T(4,128)(2,1)} %reshape.256), calls=%async_computation.3 | async-start | bytes 1310720 | tf_op jit(solution)/shard_map/all_to_all | solution.py:115
  351.9 15.9 %copy-start.1 = (bf16[1,256,5120]{2,1,0:T(8,128)(2,1)S(1)}, bf16[1,256,5120]{2,1,0:T(8,128)(2,1)}, u32[]{:S(2)}) copy-start(bf16[1,256,5120]{2,1,0:T(8,128)(2,1)} %param.19) | copy-start | bytes 7864324
Sparse Core Ops, SparseCore 0:
  32.5 156.1 all-gather.4
  191.3 74.0 all-gather.2
  267.9 74.1 reduce-scatter.1
